TPU v7x, 512 devices: a whole 4x4x16 slice. The times are simulated.
512 devices in a mesh: rows: 16 (over z_lo, x), cols: 32 (over y, z_hi, core).
Axes of the slice: x: 4, y: 4, z: 16 (z_hi: 4, z_lo: 4; z = z_hi * 4 + z_lo), core: 2. Of those that a mesh axis runs over, the one named last changes fastest.
Arguments:
- file_pixels: bfloat16 [48, 512, 4096], P(None, ('rows', 'cols')), may hold values from -6 to 6
- patchify_weight: bfloat16 [64, 48], replicated, may hold values from -0.875 to 0.875
- patchify_bias: float32 [64], replicated, may hold values from -3 to 3
- norm_gain: float32 [64], replicated, may hold values from 0.5 to 1.5
- norm_offset_vector: float32 [64], replicated, may hold values from -3 to 3
- kernel: float32 [64, 49], replicated, may hold values from -0.875 to 0.875
- kernel_offset: float32 [64], replicated, may hold values from -3 to 3
- cotangent: bfloat16 [64, 512, 4096], P(None, 'rows', 'cols'), may hold values from -10 to 10, as said below
Outputs:
- stem_output: bfloat16 [64, 512, 4096], P(None, 'rows', 'cols')
- weight_grad: float32 [64, 48], replicated
- bias_grad: float32 [64], replicated
- norm_scale_gradient: float32 [64], replicated
- shift_grad: float32 [64], replicated
- kernel_grad: float32 [64, 49], replicated
- offset_grad: float32 [64], replicated
Inputs may be any that keep to these rules, and one draw needn't show every extreme that they name: A cotangent of order one.
All inputs are finite; a program needn't handle non-finite values.
Results may differ from a plain program's by a relative error of at most 0.0055.
Values may be sent and summed in bfloat16 or wider, within the bound.
A program may use at most 64 MiB of HBM per device.

v0:
```python
import math
import jax
import jax.numpy as jnp
from jax import lax
from jax.sharding import PartitionSpec as P

norm_eps = 1e-06
side = 7


def extended(block, sides, width):
    for axis, dim in sides:
        count = lax.axis_size(axis)
        forward = [(i, i + 1) for i in range(count - 1)]
        backward = [(target, source) for source, target in forward]
        low = lax.ppermute(
            lax.slice_in_dim(block, block.shape[dim] - width, None, axis=dim), axis, forward
        )
        high = lax.ppermute(lax.slice_in_dim(block, 0, width, axis=dim), axis, backward)
        block = jnp.concatenate([low, block, high], axis=dim)
    return block


def embed_patches(pixel_values, weight, bias):
    flat = pixel_values.reshape(pixel_values.shape[0], -1)
    mixed = jnp.dot(weight, flat, preferred_element_type=jnp.float32) + bias[:, None]
    return mixed.astype(jnp.bfloat16).reshape(
        weight.shape[0], pixel_values.shape[1], pixel_values.shape[2]
    )


def apply_layer_norm(patch_embedding):
    values = patch_embedding.astype(jnp.float32)
    center = values - jnp.mean(values, axis=0, keepdims=True)
    spread = jnp.mean(center * center, axis=0, keepdims=True)
    inverse_deviation = lax.rsqrt(spread + norm_eps)
    return (center * inverse_deviation, inverse_deviation)


def depthwise(padded, taps, height, breadth):
    total = jnp.zeros((padded.shape[0], height, breadth), jnp.float32)
    for tap_row in range(side):
        for tap_col in range(side):
            window = padded[:, tap_row : tap_row + height, tap_col : tap_col + breadth].astype(
                jnp.float32
            )
            total = total + taps[:, tap_row * side + tap_col][:, None, None] * window
    return total


def kernel_terms(padded, upstream, height, breadth):
    terms = []
    for tap_row in range(side):
        for tap_col in range(side):
            window = padded[:, tap_row : tap_row + height, tap_col : tap_col + breadth].astype(
                jnp.float32
            )
            terms.append(jnp.sum(window * upstream, axis=(1, 2)))
    return jnp.stack(terms, axis=1)


def per_device(
    file_pixels,
    patchify_weight,
    patchify_bias,
    norm_gain,
    norm_offset_vector,
    kernel,
    kernel_offset,
    cotangent,
):
    height = cotangent.shape[1]
    breadth = cotangent.shape[2]
    factor = 1.0 / math.sqrt(height * lax.axis_size("rows") * breadth * lax.axis_size("cols"))
    patch_embedding = lax.all_to_all(
        embed_patches(file_pixels, patchify_weight, patchify_bias),
        "cols",
        split_axis=2,
        concat_axis=1,
        tiled=True,
    )
    centered_input, inverse_deviation = apply_layer_norm(patch_embedding)
    scale_factor = norm_gain[:, None, None]
    normalized_output = (centered_input * scale_factor + norm_offset_vector[:, None, None]).astype(
        jnp.bfloat16
    )
    tall = extended(normalized_output, (("rows", 1),), 3)
    padded = extended(tall, (("cols", 2),), 3)
    cot_tall = extended(cotangent, (("rows", 1),), 3)
    cot_pad = extended(cot_tall, (("cols", 2),), 3)
    stem_output = (
        depthwise(padded, kernel, height, breadth) + kernel_offset[:, None, None]
    ).astype(jnp.bfloat16)
    upstream = cotangent.astype(jnp.float32) * factor
    kernel_grad = kernel_terms(padded, upstream, height, breadth)
    offset_grad = jnp.sum(upstream, axis=(1, 2))
    normalized_gradient = depthwise(cot_pad, kernel[:, ::-1], height, breadth) * factor
    norm_scale_gradient = jnp.sum(normalized_gradient * centered_input, axis=(1, 2))
    shift_grad = jnp.sum(normalized_gradient, axis=(1, 2))
    input_gradient = normalized_gradient * scale_factor
    patch_gradient = inverse_deviation * (
        input_gradient
        - jnp.mean(input_gradient, axis=0, keepdims=True)
        - centered_input * jnp.mean(input_gradient * centered_input, axis=0, keepdims=True)
    )
    patch_gradient = patch_gradient.astype(jnp.bfloat16)
    local_grad = lax.all_to_all(patch_gradient, "cols", split_axis=1, concat_axis=2, tiled=True)
    partial_weight = lax.dot_general(
        local_grad.reshape(local_grad.shape[0], -1),
        file_pixels.reshape(file_pixels.shape[0], -1),
        (((1,), (1,)), ((), ())),
        preferred_element_type=jnp.float32,
    )
    bias_part = jnp.sum(local_grad.astype(jnp.float32), axis=(1, 2))
    totals = lax.psum(
        (partial_weight, bias_part, norm_scale_gradient, shift_grad, kernel_grad, offset_grad),
        ("rows", "cols"),
    )
    return (stem_output, totals[0], totals[1], totals[2], totals[3], totals[4], totals[5])


def solution(mesh):
    return jax.shard_map(
        per_device,
        mesh=mesh,
        in_specs=(
            P(None, ("rows", "cols"), None),
            P(),
            P(),
            P(),
            P(),
            P(),
            P(),
            P(None, "rows", "cols"),
        ),
        out_specs=(P(None, "rows", "cols"), P(), P(), P(), P(), P(), P()),
        check_vma=False,
    )
```

profile of v0, /device:TPU:1, one launch (start us, length us, event | category | flops | bytes accessed | tf_op | source)
XLA Modules:
  0.0 420.4 jit_solution(11450217107587844098)
XLA Ops:
  6.0 22.4 %reduce.3 = bf16[4096,64]{1,0:T(8,128)(2,1)S(1)} reduce(bf16[4096,1,64]{2,1,0:T(2,128)(2,1)S(1)} %bitcast.174, bf16[]{:T(256)} %broadcast.111), dimensions={1}, to_apply=%bitcast.163.reduce_sub_computation | reduce | bytes 1048578
  29.9 19.6 %all-to-all-start = ((bf16[32,2,4096]{2,1,0:T(2,128)(2,1)}), bf16[32,2,4096]{2,1,0:T(2,128)(2,1)}, u32[]{:S(2)}, u32[]{:S(2)}) async-start(bf16[32,2,4096]{2,1,0:T(2,128)(2,1)} %reshape.173), calls=%async_computation | async-start | bytes 1048576 | tf_op jit(solution)/shard_map/all_to_all | solution.py:75
  51.4 3.1 collective-permute-start.4
  57.6 3.3 collective-permute-done.5
  61.0 8.4 %collective-permute-start.6 = (bf16[64,38,3]{0,1,2:T(8,128)(2,1)S(1)}, bf16[64,38,3]{0,1,2:T(8,128)(2,1)S(1)}, u32[]{:S(2)}, u32[]{:S(2)}) collective-permute-start(bf16[64,38,3]{0,1,2:T(8,128)(2,1)S(1)} %get-tuple-element.117), channel_id=1, source_target_pairs={{0,1},{1,2},{2,3},{3,4},{4,5},{5,6},{6,7},{7,8},{8,9},{9,10},{10,1... | collective-permute-start | bytes 43784 | tf_op jit(solution)/shard_map/ppermute | solution.py:16
  69.4 13.0 %collective-permute-start.7 = (bf16[64,38,3]{0,1,2:T(8,128)(2,1)S(1)}, bf16[64,38,3]{0,1,2:T(8,128)(2,1)S(1)}, u32[]{:S(2)}, u32[]{:S(2)}) collective-permute-start(bf16[64,38,3]{0,1,2:T(8,128)(2,1)S(1)} %get-tuple-element.118), channel_id=1, source_target_pairs={{1,0},{2,1},{3,2},{4,3},{5,4},{6,5},{7,6},{8,7},{9,8},{10,9},{11,1... | collective-permute-start | bytes 43784 | tf_op jit(solution)/shard_map/ppermute | solution.py:19
  83.0 3.8 maximum_maximum_fusion.1
  86.8 5.5 %reshape.174 = bf16[4096,1,64]{2,1,0:T(2,128)(2,1)} reshape(bf16[32,2,4096]{2,1,0:T(2,128)(2,1)} %all-to-all-done) | data formatting | bytes 1048576
  92.3 31.6 %convert_reduce_fusion.1 = f32[4096]{0:T(1024)S(1)} fusion(bf16[4096,1,64]{2,1,0:T(2,128)(2,1)} %reshape.174), kind=kLoop, calls=%fused_computation.334 | loop fusion | flops 520192 | bytes 540672 | tf_op jit(solution)/shard_map/reduce_sum | solution.py:34
  124.0 3.3 bitcast_convert_fusion
  127.2 58.9 %multiply_reduce_fusion.2 = f32[4096]{0:T(1024)S(1)} fusion(f32[4096]{0:T(1024)S(1)} %get-tuple-element.177, bf16[4096,1,64]{2,1,0:T(2,128)(2,1)S(1)} %copy-done.3), kind=kLoop, calls=%fused_computation.233 | loop fusion | flops 1044480 | bytes 557056 | tf_op jit(solution)/shard_map/reduce_sum | solution.py:35
  186.4 22.9 %multiply_reduce_fusion = (f32[64]{0:T(128)}, f32[32,128]{0,1:T(8,128)S(1)}, f32[32,128]{0,1:T(8,128)S(1)}, f32[64]{0:T(128)}, f32[64,32,128]{0,1,2:T(8,128)S(1)}) fusion(f32[32,128]{0,1:T(8,128)S(1)} %copy.97, f32[32,128]{0,1:T(8,128)S(1)} %copy.95, f32[64,32,128]{0,2,1:T(8,128)} %bitcast.172, f32[64]{0:T(128)} %broadcast_multiply_fusion.3, ...), kind=kLoop, calls=%fused_computation.228 | loop fusion | flops 45604736 | bytes 24818688 | tf_op jit(solution)/shard_map/reduce_sum | solution.py:98
  209.3 3.5 multiply_convert_fusion
  212.9 3.1 collective-permute-start
  218.0 3.8 collective-permute-done.1
  221.8 9.0 %collective-permute-start.2 = (bf16[64,38,3]{0,1,2:T(8,128)(2,1)S(1)}, bf16[64,38,3]{0,1,2:T(8,128)(2,1)S(1)}, u32[]{:S(2)}, u32[]{:S(2)}) collective-permute-start(bf16[64,38,3]{0,1,2:T(8,128)(2,1)S(1)} %get-tuple-element.121), channel_id=1, source_target_pairs={{0,1},{1,2},{2,3},{3,4},{4,5},{5,6},{6,7},{7,8},{8,9},{9,10},{10,1... | collective-permute-start | bytes 43784 | tf_op jit(solution)/shard_map/ppermute | solution.py:16
  234.6 14.7 %all-to-all-start.1 = ((bf16[64,32,128]{2,0,1:T(8,128)(2,1)}), bf16[64,32,128]{2,0,1:T(8,128)(2,1)S(1)}, u32[]{:S(2)}, u32[]{:S(2)}) async-start(bf16[64,32,128]{2,0,1:T(8,128)(2,1)} %copy.104), calls=%async_computation.1 | async-start | bytes 1048576 | tf_op jit(solution)/shard_map/all_to_all | solution.py:107
  249.4 4.1 maximum_maximum_fusion
  253.9 7.2 %fusion.148 = (f32[64]{0:T(128)}, f32[64]{0:T(128)}, f32[64]{0:T(128)}, f32[64]{0:T(128)}, f32[64]{0:T(128)}, /*index=5*/f32[64]{0:T(128)}, f32[64]{0:T(128)}, f...) fusion(bf16[64,32,128]{0,1,2:T(8,128)(2,1)S(1)} %copy-done.2, ...), kind=kLoop, calls=%fused_computation.200 | loop fusion | flops 14678912 | bytes 9966080 | tf_op jit(solution)/shard_map/reduce_sum | solution.py:58
  261.5 17.8 %add_convert_fusion = bf16[64,32,128]{0,1,2:T(8,128)(2,1)} fusion(bf16[64,32,128]{0,1,2:T(8,128)(2,1)S(1)} %copy-done.5, bf16[64,3,128]{0,1,2:T(4,128)(2,1)S(1)} %copy-done.8, bf16[64,3,128]{0,1,2:T(4,128)(2,1)S(1)} %collective-permute-done, f32[64]{0:T(128)} %param.14, f32[64]{0:T(128)S(1)} %copy-done.50, f32[64]{0:T(128)S(1)} %copy-done.51, ...), kind=kLoop, calls=%fused_computation.231 | loop fusion | flops 43515904 | bytes 23179776 | tf_op jit(solution)/shard_map/convert_element_type | solution.py:93
  279.3 4.6 %fusion.147 = (f32[64]{0:T(128)S(1)}, f32[64]{0:T(128)S(1)}, f32[64]{0:T(128)S(1)}, f32[64]{0:T(128)S(1)}, f32[64]{0:T(128)S(1)}, /*index=5*/f32[64]{0:T(128)S(1...) fusion(bf16[64,32,128]{0,1,2:T(8,128)(2,1)S(1)} %copy-done.2, ...), kind=kLoop, calls=%fused_computation.199 | loop fusion | flops 13106560 | bytes 2722304 | tf_op jit(solution)/shard_map/reduce_sum | solution.py:58
  283.9 3.6 copy.106
  288.5 6.8 %fusion.144 = (f32[64]{0:T(128)S(1)}, f32[64]{0:T(128)S(1)}, f32[64]{0:T(128)S(1)}, f32[64]{0:T(128)S(1)}, f32[64]{0:T(128)S(1)}, /*index=5*/f32[64]{0:T(128)S(1...) fusion(bf16[64,32,128]{0,1,2:T(8,128)(2,1)S(1)} %copy-done.2, ...), kind=kLoop, calls=%fused_computation.196 | loop fusion | flops 14940992 | bytes 9966336 | tf_op jit(solution)/shard_map/reduce_sum | solution.py:58
  296.1 123.9 %all-reduce = (f32[64,48]{0,1:T(8,128)}, f32[64]{0:T(128)}, f32[64]{0:T(128)}, f32[64]{0:T(128)}, f32[64,49]{0,1:T(8,128)}, /*index=5*/f32[64]{0:T(128)}) all-reduce(f32[64,48]{0,1:T(8,128)S(1)} %fusion.183, f32[64]{0:T(128)S(1)} %convert_reduce_fusion, f32[64]{0:T(128)S(1)} %copy-done.70, ...), channel_id=1, replica_groups=mesh['rows'=16,'cols'=32] {'rows','cols'}, use_global_device_ids=true, to_apply=%region_4.0 | all-reduce | flops 6464 | bytes 51712 | tf_op jit(solution)/shard_map/psum | solution.py:115
  (186 shorter events, 20.2 us)
Async XLA Ops:
  28.4 21.1 %copy-start.9 = (bf16[64,32,128]{2,1,0:T(8,128)(2,1)S(1)}, bf16[64,32,128]{2,1,0:T(8,128)(2,1)}, u32[]{:S(2)}) copy-start(bf16[64,32,128]{2,1,0:T(8,128)(2,1)} %param.15) | copy-start | bytes 1572868
  28.4 27.4 %copy-start.10 = (f32[64,49]{0,1:T(8,128)S(1)}, f32[64,49]{0,1:T(8,128)}, u32[]{:S(2)}) copy-start(f32[64,49]{0,1:T(8,128)} %param.13) | copy-start | bytes 37636
  29.9 52.5 %copy-start.73 = (f32[64]{0:T(128)S(1)}, f32[64]{0:T(128)}, u32[]{:S(2)}) copy-start(f32[64]{0:T(128)} %param.11) | copy-start | bytes 772
  29.9 56.8 %all-to-all-start = ((bf16[32,2,4096]{2,1,0:T(2,128)(2,1)}), bf16[32,2,4096]{2,1,0:T(2,128)(2,1)}, u32[]{:S(2)}, u32[]{:S(2)}) async-start(bf16[32,2,4096]{2,1,0:T(2,128)(2,1)} %reshape.173), calls=%async_computation | async-start | bytes 1048576 | tf_op jit(solution)/shard_map/all_to_all | solution.py:75
  51.2 31.7 %copy-start.1 = (bf16[64,32,128]{0,1,2:T(8,128)(2,1)}, bf16[64,32,128]{0,1,2:T(8,128)(2,1)S(1)}, u32[]{:S(2)}) copy-start(bf16[64,32,128]{0,1,2:T(8,128)(2,1)S(1)} %copy.98) | copy-start | bytes 1572868
  51.4 6.3 %collective-permute-start.4 = (bf16[64,3,128]{0,1,2:T(4,128)(2,1)S(1)}, bf16[64,3,128]{0,1,2:T(4,128)(2,1)S(1)}, u32[]{:S(2)}, u32[]{:S(2)}) collective-permute-start(bf16[64,3,128]{0,1,2:T(4,128)(2,1)S(1)} %get-tuple-element.123), channel_id=1, source_target_pairs={{0,32},{32,64},{64,96},{96,128},{128,160},{160,192},{192,224},{224... | collective-permute-start | bytes 147464 | tf_op jit(solution)/shard_map/ppermute | solution.py:16
  54.5 6.5 %collective-permute-start.5 = (bf16[64,3,128]{0,1,2:T(4,128)(2,1)S(1)}, bf16[64,3,128]{0,1,2:T(4,128)(2,1)S(1)}, u32[]{:S(2)}, u32[]{:S(2)}) collective-permute-start(bf16[64,3,128]{0,1,2:T(4,128)(2,1)S(1)} %get-tuple-element.124), channel_id=1, source_target_pairs={{32,0},{64,32},{96,64},{128,96},{160,128},{192,160},{224,192},{256... | collective-permute-start | bytes 147464 | tf_op jit(solution)/shard_map/ppermute | solution.py:19
  56.3 130.0 %copy-start.11 = (f32[64]{0:T(128)}, f32[64]{0:T(128)S(1)}, u32[]{:S(2)}) copy-start(f32[64]{0:T(128)S(1)} %get-tuple-element.139) | copy-start | bytes 772
  56.3 130.0 %copy-start.13 = (f32[64]{0:T(128)}, f32[64]{0:T(128)S(1)}, u32[]{:S(2)}) copy-start(f32[64]{0:T(128)S(1)} %get-tuple-element.140) | copy-start | bytes 772
  56.3 130.0 %copy-start.15 = (f32[64]{0:T(128)}, f32[64]{0:T(128)S(1)}, u32[]{:S(2)}) copy-start(f32[64]{0:T(128)S(1)} %get-tuple-element.141) | copy-start | bytes 772
  56.3 130.0 %copy-start.17 = (f32[64]{0:T(128)}, f32[64]{0:T(128)S(1)}, u32[]{:S(2)}) copy-start(f32[64]{0:T(128)S(1)} %get-tuple-element.142) | copy-start | bytes 772
  61.0 22.0 %collective-permute-start.6 = (bf16[64,38,3]{0,1,2:T(8,128)(2,1)S(1)}, bf16[64,38,3]{0,1,2:T(8,128)(2,1)S(1)}, u32[]{:S(2)}, u32[]{:S(2)}) collective-permute-start(bf16[64,38,3]{0,1,2:T(8,128)(2,1)S(1)} %get-tuple-element.117), channel_id=1, source_target_pairs={{0,1},{1,2},{2,3},{3,4},{4,5},{5,6},{6,7},{7,8},{8,9},{9,10},{10,1... | collective-permute-start | bytes 43784 | tf_op jit(solution)/shard_map/ppermute | solution.py:16
  69.4 13.5 %collective-permute-start.7 = (bf16[64,38,3]{0,1,2:T(8,128)(2,1)S(1)}, bf16[64,38,3]{0,1,2:T(8,128)(2,1)S(1)}, u32[]{:S(2)}, u32[]{:S(2)}) collective-permute-start(bf16[64,38,3]{0,1,2:T(8,128)(2,1)S(1)} %get-tuple-element.118), channel_id=1, source_target_pairs={{1,0},{2,1},{3,2},{4,3},{5,4},{6,5},{7,6},{8,7},{9,8},{10,9},{11,1... | collective-permute-start | bytes 43784 | tf_op jit(solution)/shard_map/ppermute | solution.py:19
  92.3 31.7 %copy-start.3 = (bf16[4096,1,64]{2,1,0:T(2,128)(2,1)S(1)}, bf16[4096,1,64]{2,1,0:T(2,128)(2,1)}, u32[]{:S(2)}) copy-start(bf16[4096,1,64]{2,1,0:T(2,128)(2,1)} %reshape.174) | copy-start | bytes 1572868
  186.4 22.9 %copy-start.6 = (f32[64,1,4096]{0,1,2:T(1,128)S(1)}, f32[64,1,4096]{0,1,2:T(1,128)}, u32[]{:S(2)}) copy-start(f32[64,1,4096]{0,1,2:T(1,128)} %bitcast_convert_fusion) | copy-start | bytes 3145732
  186.4 22.9 %copy-start.72 = (f32[64]{0:T(128)S(1)}, f32[64]{0:T(128)}, u32[]{:S(2)}) copy-start(f32[64]{0:T(128)} %broadcast_multiply_fusion.3) | copy-start | bytes 772
  186.4 22.9 %copy-start.74 = (f32[64]{0:T(128)S(1)}, f32[64]{0:T(128)}, u32[]{:S(2)}) copy-start(f32[64]{0:T(128)} %param.11) | copy-start | bytes 772
  186.4 22.9 %copy-start.75 = (f32[64]{0:T(128)S(1)}, f32[64]{0:T(128)}, u32[]{:S(2)}) copy-start(f32[64]{0:T(128)} %param.12) | copy-start | bytes 772
  212.9 5.1 %collective-permute-start = (bf16[64,3,128]{0,1,2:T(4,128)(2,1)S(1)}, bf16[64,3,128]{0,1,2:T(4,128)(2,1)S(1)}, u32[]{:S(2)}, u32[]{:S(2)}) collective-permute-start(bf16[64,3,128]{0,1,2:T(4,128)(2,1)S(1)} %get-tuple-element.125), channel_id=1, source_target_pairs={{0,32},{32,64},{64,96},{96,128},{128,160},{160,192},{192,224},{224... | collective-permute-start | bytes 147464 | tf_op jit(solution)/shard_map/ppermute | solution.py:16
  216.1 5.7 %collective-permute-start.1 = (bf16[64,3,128]{0,1,2:T(4,128)(2,1)S(1)}, bf16[64,3,128]{0,1,2:T(4,128)(2,1)S(1)}, u32[]{:S(2)}, u32[]{:S(2)}) collective-permute-start(bf16[64,3,128]{0,1,2:T(4,128)(2,1)S(1)} %get-tuple-element.126), channel_id=1, source_target_pairs={{32,0},{64,32},{96,64},{128,96},{160,128},{192,160},{224,192},{256... | collective-permute-start | bytes 147464 | tf_op jit(solution)/shard_map/ppermute | solution.py:19
  221.8 27.6 %copy-start.7 = (bf16[64,3,128]{0,1,2:T(4,128)(2,1)}, bf16[64,3,128]{0,1,2:T(4,128)(2,1)S(1)}, u32[]{:S(2)}) copy-start(bf16[64,3,128]{0,1,2:T(4,128)(2,1)S(1)} %collective-permute-done.1) | copy-start | bytes 147460
  221.8 27.5 %collective-permute-start.2 = (bf16[64,38,3]{0,1,2:T(8,128)(2,1)S(1)}, bf16[64,38,3]{0,1,2:T(8,128)(2,1)S(1)}, u32[]{:S(2)}, u32[]{:S(2)}) collective-permute-start(bf16[64,38,3]{0,1,2:T(8,128)(2,1)S(1)} %get-tuple-element.121), channel_id=1, source_target_pairs={{0,1},{1,2},{2,3},{3,4},{4,5},{5,6},{6,7},{7,8},{8,9},{9,10},{10,1... | collective-permute-start | bytes 43784 | tf_op jit(solution)/shard_map/ppermute | solution.py:16
  230.8 18.6 %collective-permute-start.3 = (bf16[64,38,3]{0,1,2:T(8,128)(2,1)S(1)}, bf16[64,38,3]{0,1,2:T(8,128)(2,1)S(1)}, u32[]{:S(2)}, u32[]{:S(2)}) collective-permute-start(bf16[64,38,3]{0,1,2:T(8,128)(2,1)S(1)} %get-tuple-element.122), channel_id=1, source_target_pairs={{1,0},{2,1},{3,2},{4,3},{5,4},{6,5},{7,6},{8,7},{9,8},{10,9},{11,1... | collective-permute-start | bytes 43784 | tf_op jit(solution)/shard_map/ppermute | solution.py:19
  234.6 61.0 %all-to-all-start.1 = ((bf16[64,32,128]{2,0,1:T(8,128)(2,1)}), bf16[64,32,128]{2,0,1:T(8,128)(2,1)S(1)}, u32[]{:S(2)}, u32[]{:S(2)}) async-start(bf16[64,32,128]{2,0,1:T(8,128)(2,1)} %copy.104), calls=%async_computation.1 | async-start | bytes 1048576 | tf_op jit(solution)/shard_map/all_to_all | solution.py:107
  (62 other events, 451.4 us)
where the time goes:
time: 428 us; the launch traced here: 420 us
  other arithmetic  188 us (44%)
  blocking collectives  124 us (29%)
  starting transfers between devices  75.4 us (18%)
  local copies, waits for them, and re-layouts  21.3 us (5%)
  waiting for transfers between devices  7.75 us (2%)
    psum x1, blocking collectives, per_device(): lax.psum((partial_weight, bias_part, norm_scale_gradient, shift_grad, ker...  124 us
    reduce_sum x1, other arithmetic, apply_layer_norm(): spread = jnp.mean(center * center, axis=0, keepdims=True)  58.9 us
    reduce_sum x1, other arithmetic, apply_layer_norm(): center = values - jnp.mean(values, axis=0, keepdims=True)  31.6 us
    ppermute x4, starting transfers between devices, extended(): lax.ppermute(lax.slice_in_dim(block, block.shape[dim] - width, None, axis...  23.7 us
    reduce_sum x1, other arithmetic, per_device(): jnp.sum(normalized_gradient * centered_input, axis=(1, 2))  22.9 us
    unnamed x1, other arithmetic  22.4 us
    all_to_all x1, starting transfers between devices, per_device(): lax.all_to_all(embed_patches(file_pixels, patchify_weight, patchify_bias)...  19.6 us
    reduce_sum x4, other arithmetic, kernel_terms(): terms.append(jnp.sum(window * upstream, axis=(1, 2)))  19.4 us
  transfers between devices with their start and end apart: 10, of which 3 were waited for; matrix products, arithmetic and copies ran while one was open for 13% of the time, Pallas kernels for 0%

commit v1 on v0

--- a/solution.py
+++ b/solution.py
@@ -113,8 +113,11 @@
     )
     bias_part = jnp.sum(local_grad.astype(jnp.float32), axis=(1, 2))
     totals = lax.psum(
-        (partial_weight, bias_part, norm_scale_gradient, shift_grad, kernel_grad, offset_grad),
-        ("rows", "cols"),
+        lax.psum(
+            (partial_weight, bias_part, norm_scale_gradient, shift_grad, kernel_grad, offset_grad),
+            "rows",
+        ),
+        "cols",
     )
     return (stem_output, totals[0], totals[1], totals[2], totals[3], totals[4], totals[5])
 

time: 428 us -> 556 us (1.30)
  blocking collectives: 124 us -> 249 us
    psum x0 -> x1, blocking collectives: none -> 173 us  [per_device(): lax.psum(lax.psum((partial_weight, bias_part, norm_scale_gradient, shift_...]
    psum x1, blocking collectives: 124 us -> 76.2 us  [per_device(): lax.psum((partial_weight, bias_part, norm_scale_gradient, shift_grad, ker...]
  transfers between devices with their start and end apart: 10 -> 10, of which waited for: 3 -> 3; matrix products, arithmetic and copies ran while one was open for 13% -> 10% of each run, Pallas kernels for 0% -> 0%
where the time goes in v1:
time: 556 us; the launch traced here: 546 us
  blocking collectives  249 us (45%)
  other arithmetic  188 us (34%)
  starting transfers between devices  75.4 us (14%)
  local copies, waits for them, and re-layouts  21.3 us (4%)
  waiting for transfers between devices  7.75 us (1%)
    psum x1, blocking collectives, per_device(): lax.psum(lax.psum((partial_weight, bias_part, norm_scale_gradient, shift_...  173 us
    psum x1, blocking collectives, per_device(): lax.psum((partial_weight, bias_part, norm_scale_gradient, shift_grad, ker...  76.2 us
    reduce_sum x1, other arithmetic, apply_layer_norm(): spread = jnp.mean(center * center, axis=0, keepdims=True)  58.9 us
    reduce_sum x1, other arithmetic, apply_layer_norm(): center = values - jnp.mean(values, axis=0, keepdims=True)  31.6 us
    ppermute x4, starting transfers between devices, extended(): lax.ppermute(lax.slice_in_dim(block, block.shape[dim] - width, None, axis...  23.7 us
    reduce_sum x1, other arithmetic, per_device(): jnp.sum(normalized_gradient * centered_input, axis=(1, 2))  22.9 us
    unnamed x1, other arithmetic  22.4 us
    all_to_all x1, starting transfers between devices, per_device(): lax.all_to_all(embed_patches(file_pixels, patchify_weight, patchify_bias)...  19.6 us
  transfers between devices with their start and end apart: 10, of which 3 were waited for; matrix products, arithmetic and copies ran while one was open for 10% of the time, Pallas kernels for 0%

profile of v1, /device:TPU:1, one launch (start us, length us, event | category | flops | bytes accessed | tf_op | source)
XLA Modules:
  0.0 545.9 jit_solution(17327273481336774534)
XLA Ops:
  6.0 22.4 %reduce.3 = bf16[4096,64]{1,0:T(8,128)(2,1)S(1)} reduce(bf16[4096,1,64]{2,1,0:T(2,128)(2,1)S(1)} %bitcast.174, bf16[]{:T(256)} %broadcast.111), dimensions={1}, to_apply=%bitcast.163.reduce_sub_computation | reduce | bytes 1048578
  29.9 19.6 %all-to-all-start = ((bf16[32,2,4096]{2,1,0:T(2,128)(2,1)}), bf16[32,2,4096]{2,1,0:T(2,128)(2,1)}, u32[]{:S(2)}, u32[]{:S(2)}) async-start(bf16[32,2,4096]{2,1,0:T(2,128)(2,1)} %reshape.173), calls=%async_computation | async-start | bytes 1048576 | tf_op jit(solution)/shard_map/all_to_all | solution.py:75
  51.4 3.1 collective-permute-start.4
  57.6 3.3 collective-permute-done.5
  61.0 8.4 %collective-permute-start.6 = (bf16[64,38,3]{0,1,2:T(8,128)(2,1)S(1)}, bf16[64,38,3]{0,1,2:T(8,128)(2,1)S(1)}, u32[]{:S(2)}, u32[]{:S(2)}) collective-permute-start(bf16[64,38,3]{0,1,2:T(8,128)(2,1)S(1)} %get-tuple-element.123), channel_id=1, source_target_pairs={{0,1},{1,2},{2,3},{3,4},{4,5},{5,6},{6,7},{7,8},{8,9},{9,10},{10,1... | collective-permute-start | bytes 43784 | tf_op jit(solution)/shard_map/ppermute | solution.py:16
  69.4 13.0 %collective-permute-start.7 = (bf16[64,38,3]{0,1,2:T(8,128)(2,1)S(1)}, bf16[64,38,3]{0,1,2:T(8,128)(2,1)S(1)}, u32[]{:S(2)}, u32[]{:S(2)}) collective-permute-start(bf16[64,38,3]{0,1,2:T(8,128)(2,1)S(1)} %get-tuple-element.124), channel_id=1, source_target_pairs={{1,0},{2,1},{3,2},{4,3},{5,4},{6,5},{7,6},{8,7},{9,8},{10,9},{11,1... | collective-permute-start | bytes 43784 | tf_op jit(solution)/shard_map/ppermute | solution.py:19
  83.0 3.8 maximum_maximum_fusion.1
  86.8 5.5 %reshape.174 = bf16[4096,1,64]{2,1,0:T(2,128)(2,1)} reshape(bf16[32,2,4096]{2,1,0:T(2,128)(2,1)} %all-to-all-done) | data formatting | bytes 1048576
  92.3 31.6 %convert_reduce_fusion.1 = f32[4096]{0:T(1024)S(1)} fusion(bf16[4096,1,64]{2,1,0:T(2,128)(2,1)} %reshape.174), kind=kLoop, calls=%fused_computation.334 | loop fusion | flops 520192 | bytes 540672 | tf_op jit(solution)/shard_map/reduce_sum | solution.py:34
  124.0 3.3 bitcast_convert_fusion
  127.2 58.9 %multiply_reduce_fusion.2 = f32[4096]{0:T(1024)S(1)} fusion(f32[4096]{0:T(1024)S(1)} %get-tuple-element.183, bf16[4096,1,64]{2,1,0:T(2,128)(2,1)S(1)} %copy-done.3), kind=kLoop, calls=%fused_computation.233 | loop fusion | flops 1044480 | bytes 557056 | tf_op jit(solution)/shard_map/reduce_sum | solution.py:35
  186.4 22.9 %multiply_reduce_fusion = (f32[64]{0:T(128)}, f32[32,128]{0,1:T(8,128)S(1)}, f32[32,128]{0,1:T(8,128)S(1)}, f32[64]{0:T(128)}, f32[64,32,128]{0,1,2:T(8,128)S(1)}) fusion(f32[32,128]{0,1:T(8,128)S(1)} %copy.97, f32[32,128]{0,1:T(8,128)S(1)} %copy.95, f32[64,32,128]{0,2,1:T(8,128)} %bitcast.172, f32[64]{0:T(128)} %broadcast_multiply_fusion.3, ...), kind=kLoop, calls=%fused_computation.228 | loop fusion | flops 45604736 | bytes 24818688 | tf_op jit(solution)/shard_map/reduce_sum | solution.py:98
  209.3 3.5 multiply_convert_fusion
  218.0 3.8 collective-permute-done.1
  221.8 9.0 %collective-permute-start.2 = (bf16[64,38,3]{0,1,2:T(8,128)(2,1)S(1)}, bf16[64,38,3]{0,1,2:T(8,128)(2,1)S(1)}, u32[]{:S(2)}, u32[]{:S(2)}) collective-permute-start(bf16[64,38,3]{0,1,2:T(8,128)(2,1)S(1)} %get-tuple-element.127), channel_id=1, source_target_pairs={{0,1},{1,2},{2,3},{3,4},{4,5},{5,6},{6,7},{7,8},{8,9},{9,10},{10,1... | collective-permute-start | bytes 43784 | tf_op jit(solution)/shard_map/ppermute | solution.py:16
  234.6 14.7 %all-to-all-start.1 = ((bf16[64,32,128]{2,0,1:T(8,128)(2,1)}), bf16[64,32,128]{2,0,1:T(8,128)(2,1)S(1)}, u32[]{:S(2)}, u32[]{:S(2)}) async-start(bf16[64,32,128]{2,0,1:T(8,128)(2,1)} %copy.104), calls=%async_computation.1 | async-start | bytes 1048576 | tf_op jit(solution)/shard_map/all_to_all | solution.py:107
  249.4 4.1 maximum_maximum_fusion
  253.9 7.2 %fusion.148 = (f32[64]{0:T(128)}, f32[64]{0:T(128)}, f32[64]{0:T(128)}, f32[64]{0:T(128)}, f32[64]{0:T(128)}, /*index=5*/f32[64]{0:T(128)}, f32[64]{0:T(128)}, f...) fusion(bf16[64,32,128]{0,1,2:T(8,128)(2,1)S(1)} %copy-done.2, ...), kind=kLoop, calls=%fused_computation.200 | loop fusion | flops 14678912 | bytes 9966080 | tf_op jit(solution)/shard_map/reduce_sum | solution.py:58
  261.5 17.8 %add_convert_fusion = bf16[64,32,128]{0,1,2:T(8,128)(2,1)} fusion(bf16[64,32,128]{0,1,2:T(8,128)(2,1)S(1)} %copy-done.5, bf16[64,3,128]{0,1,2:T(4,128)(2,1)S(1)} %copy-done.8, bf16[64,3,128]{0,1,2:T(4,128)(2,1)S(1)} %collective-permute-done, f32[64]{0:T(128)} %param.14, f32[64]{0:T(128)S(1)} %copy-done.50, f32[64]{0:T(128)S(1)} %copy-done.51, ...), kind=kLoop, calls=%fused_computation.231 | loop fusion | flops 43515904 | bytes 23179776 | tf_op jit(solution)/shard_map/convert_element_type | solution.py:93
  279.3 4.6 fusion.147
  283.9 3.6 copy.106
  288.5 6.8 %fusion.144 = (f32[64]{0:T(128)S(1)}, f32[64]{0:T(128)S(1)}, f32[64]{0:T(128)S(1)}, f32[64]{0:T(128)S(1)}, f32[64]{0:T(128)S(1)}, /*index=5*/f32[64]{0:T(128)S(1...) fusion(bf16[64,32,128]{0,1,2:T(8,128)(2,1)S(1)} %copy-done.2, ...), kind=kLoop, calls=%fused_computation.196 | loop fusion | flops 14940992 | bytes 9966336 | tf_op jit(solution)/shard_map/reduce_sum | solution.py:58
  296.1 76.2 %all-reduce.1 = (f32[64,48]{0,1:T(8,128)S(1)}, f32[64]{0:T(128)S(1)}, f32[64]{0:T(128)S(1)}, f32[64]{0:T(128)S(1)}, f32[64,49]{0,1:T(8,128)S(1)}, /*index=5*/f32[64]{0:T(128)S(1)}) all-reduce(f32[64,48]{0,1:T(8,128)S(1)} %fusion.183, f32[64]{0:T(128)S(1)} %convert_reduce_fusion, ...), channel_id=1, replica_groups=mesh['rows'=16,'cols'=32] {'rows'}, use_global_device_ids=true, to_apply=%region_4.0 | all-reduce | flops 6464 | bytes 51712 | tf_op jit(solution)/shard_map/psum | solution.py:116
  372.4 173.1 %all-reduce = (f32[64,48]{0,1:T(8,128)}, f32[64]{0:T(128)}, f32[64]{0:T(128)}, f32[64]{0:T(128)}, f32[64,49]{0,1:T(8,128)}, /*index=5*/f32[64]{0:T(128)}) all-reduce(f32[64,48]{0,1:T(8,128)S(1)} %get-tuple-element.112, f32[64]{0:T(128)S(1)} %get-tuple-element.113, ...), channel_id=1, replica_groups=mesh['rows'=16,'cols'=32] {'cols'}, use_global_device_ids=true, to_apply=%region_5.0 | all-reduce | flops 6464 | bytes 51712 | tf_op jit(solution)/shard_map/psum | solution.py:115
  (187 shorter events, 23.3 us)
Async XLA Ops:
  28.4 21.1 %copy-start.9 = (bf16[64,32,128]{2,1,0:T(8,128)(2,1)S(1)}, bf16[64,32,128]{2,1,0:T(8,128)(2,1)}, u32[]{:S(2)}) copy-start(bf16[64,32,128]{2,1,0:T(8,128)(2,1)} %param.15) | copy-start | bytes 1572868
  28.4 27.4 %copy-start.10 = (f32[64,49]{0,1:T(8,128)S(1)}, f32[64,49]{0,1:T(8,128)}, u32[]{:S(2)}) copy-start(f32[64,49]{0,1:T(8,128)} %param.13) | copy-start | bytes 37636
  29.9 52.5 %copy-start.73 = (f32[64]{0:T(128)S(1)}, f32[64]{0:T(128)}, u32[]{:S(2)}) copy-start(f32[64]{0:T(128)} %param.11) | copy-start | bytes 772
  29.9 56.8 %all-to-all-start = ((bf16[32,2,4096]{2,1,0:T(2,128)(2,1)}), bf16[32,2,4096]{2,1,0:T(2,128)(2,1)}, u32[]{:S(2)}, u32[]{:S(2)}) async-start(bf16[32,2,4096]{2,1,0:T(2,128)(2,1)} %reshape.173), calls=%async_computation | async-start | bytes 1048576 | tf_op jit(solution)/shard_map/all_to_all | solution.py:75
  51.2 31.7 %copy-start.1 = (bf16[64,32,128]{0,1,2:T(8,128)(2,1)}, bf16[64,32,128]{0,1,2:T(8,128)(2,1)S(1)}, u32[]{:S(2)}) copy-start(bf16[64,32,128]{0,1,2:T(8,128)(2,1)S(1)} %copy.98) | copy-start | bytes 1572868
  51.4 6.3 %collective-permute-start.4 = (bf16[64,3,128]{0,1,2:T(4,128)(2,1)S(1)}, bf16[64,3,128]{0,1,2:T(4,128)(2,1)S(1)}, u32[]{:S(2)}, u32[]{:S(2)}) collective-permute-start(bf16[64,3,128]{0,1,2:T(4,128)(2,1)S(1)} %get-tuple-element.129), channel_id=1, source_target_pairs={{0,32},{32,64},{64,96},{96,128},{128,160},{160,192},{192,224},{224... | collective-permute-start | bytes 147464 | tf_op jit(solution)/shard_map/ppermute | solution.py:16
  54.5 6.5 %collective-permute-start.5 = (bf16[64,3,128]{0,1,2:T(4,128)(2,1)S(1)}, bf16[64,3,128]{0,1,2:T(4,128)(2,1)S(1)}, u32[]{:S(2)}, u32[]{:S(2)}) collective-permute-start(bf16[64,3,128]{0,1,2:T(4,128)(2,1)S(1)} %get-tuple-element.130), channel_id=1, source_target_pairs={{32,0},{64,32},{96,64},{128,96},{160,128},{192,160},{224,192},{256... | collective-permute-start | bytes 147464 | tf_op jit(solution)/shard_map/ppermute | solution.py:19
  56.3 130.0 %copy-start.11 = (f32[64]{0:T(128)}, f32[64]{0:T(128)S(1)}, u32[]{:S(2)}) copy-start(f32[64]{0:T(128)S(1)} %get-tuple-element.145) | copy-start | bytes 772
  56.3 130.0 %copy-start.13 = (f32[64]{0:T(128)}, f32[64]{0:T(128)S(1)}, u32[]{:S(2)}) copy-start(f32[64]{0:T(128)S(1)} %get-tuple-element.146) | copy-start | bytes 772
  56.3 130.0 %copy-start.15 = (f32[64]{0:T(128)}, f32[64]{0:T(128)S(1)}, u32[]{:S(2)}) copy-start(f32[64]{0:T(128)S(1)} %get-tuple-element.147) | copy-start | bytes 772
  56.3 130.0 %copy-start.17 = (f32[64]{0:T(128)}, f32[64]{0:T(128)S(1)}, u32[]{:S(2)}) copy-start(f32[64]{0:T(128)S(1)} %get-tuple-element.148) | copy-start | bytes 772
  61.0 22.0 %collective-permute-start.6 = (bf16[64,38,3]{0,1,2:T(8,128)(2,1)S(1)}, bf16[64,38,3]{0,1,2:T(8,128)(2,1)S(1)}, u32[]{:S(2)}, u32[]{:S(2)}) collective-permute-start(bf16[64,38,3]{0,1,2:T(8,128)(2,1)S(1)} %get-tuple-element.123), channel_id=1, source_target_pairs={{0,1},{1,2},{2,3},{3,4},{4,5},{5,6},{6,7},{7,8},{8,9},{9,10},{10,1... | collective-permute-start | bytes 43784 | tf_op jit(solution)/shard_map/ppermute | solution.py:16
  69.4 13.5 %collective-permute-start.7 = (bf16[64,38,3]{0,1,2:T(8,128)(2,1)S(1)}, bf16[64,38,3]{0,1,2:T(8,128)(2,1)S(1)}, u32[]{:S(2)}, u32[]{:S(2)}) collective-permute-start(bf16[64,38,3]{0,1,2:T(8,128)(2,1)S(1)} %get-tuple-element.124), channel_id=1, source_target_pairs={{1,0},{2,1},{3,2},{4,3},{5,4},{6,5},{7,6},{8,7},{9,8},{10,9},{11,1... | collective-permute-start | bytes 43784 | tf_op jit(solution)/shard_map/ppermute | solution.py:19
  92.3 31.7 %copy-start.3 = (bf16[4096,1,64]{2,1,0:T(2,128)(2,1)S(1)}, bf16[4096,1,64]{2,1,0:T(2,128)(2,1)}, u32[]{:S(2)}) copy-start(bf16[4096,1,64]{2,1,0:T(2,128)(2,1)} %reshape.174) | copy-start | bytes 1572868
  186.4 22.9 %copy-start.6 = (f32[64,1,4096]{0,1,2:T(1,128)S(1)}, f32[64,1,4096]{0,1,2:T(1,128)}, u32[]{:S(2)}) copy-start(f32[64,1,4096]{0,1,2:T(1,128)} %bitcast_convert_fusion) | copy-start | bytes 3145732
  186.4 22.9 %copy-start.72 = (f32[64]{0:T(128)S(1)}, f32[64]{0:T(128)}, u32[]{:S(2)}) copy-start(f32[64]{0:T(128)} %broadcast_multiply_fusion.3) | copy-start | bytes 772
  186.4 22.9 %copy-start.74 = (f32[64]{0:T(128)S(1)}, f32[64]{0:T(128)}, u32[]{:S(2)}) copy-start(f32[64]{0:T(128)} %param.11) | copy-start | bytes 772
  186.4 22.9 %copy-start.75 = (f32[64]{0:T(128)S(1)}, f32[64]{0:T(128)}, u32[]{:S(2)}) copy-start(f32[64]{0:T(128)} %param.12) | copy-start | bytes 772
  212.9 5.1 collective-permute-start
  216.1 5.7 %collective-permute-start.1 = (bf16[64,3,128]{0,1,2:T(4,128)(2,1)S(1)}, bf16[64,3,128]{0,1,2:T(4,128)(2,1)S(1)}, u32[]{:S(2)}, u32[]{:S(2)}) collective-permute-start(bf16[64,3,128]{0,1,2:T(4,128)(2,1)S(1)} %get-tuple-element.132), channel_id=1, source_target_pairs={{32,0},{64,32},{96,64},{128,96},{160,128},{192,160},{224,192},{256... | collective-permute-start | bytes 147464 | tf_op jit(solution)/shard_map/ppermute | solution.py:19
  221.8 27.6 %copy-start.7 = (bf16[64,3,128]{0,1,2:T(4,128)(2,1)}, bf16[64,3,128]{0,1,2:T(4,128)(2,1)S(1)}, u32[]{:S(2)}) copy-start(bf16[64,3,128]{0,1,2:T(4,128)(2,1)S(1)} %collective-permute-done.1) | copy-start | bytes 147460
  221.8 27.5 %collective-permute-start.2 = (bf16[64,38,3]{0,1,2:T(8,128)(2,1)S(1)}, bf16[64,38,3]{0,1,2:T(8,128)(2,1)S(1)}, u32[]{:S(2)}, u32[]{:S(2)}) collective-permute-start(bf16[64,38,3]{0,1,2:T(8,128)(2,1)S(1)} %get-tuple-element.127), channel_id=1, source_target_pairs={{0,1},{1,2},{2,3},{3,4},{4,5},{5,6},{6,7},{7,8},{8,9},{9,10},{10,1... | collective-permute-start | bytes 43784 | tf_op jit(solution)/shard_map/ppermute | solution.py:16
  230.8 18.6 %collective-permute-start.3 = (bf16[64,38,3]{0,1,2:T(8,128)(2,1)S(1)}, bf16[64,38,3]{0,1,2:T(8,128)(2,1)S(1)}, u32[]{:S(2)}, u32[]{:S(2)}) collective-permute-start(bf16[64,38,3]{0,1,2:T(8,128)(2,1)S(1)} %get-tuple-element.128), channel_id=1, source_target_pairs={{1,0},{2,1},{3,2},{4,3},{5,4},{6,5},{7,6},{8,7},{9,8},{10,9},{11,1... | collective-permute-start | bytes 43784 | tf_op jit(solution)/shard_map/ppermute | solution.py:19
  234.6 61.0 %all-to-all-start.1 = ((bf16[64,32,128]{2,0,1:T(8,128)(2,1)}), bf16[64,32,128]{2,0,1:T(8,128)(2,1)S(1)}, u32[]{:S(2)}, u32[]{:S(2)}) async-start(bf16[64,32,128]{2,0,1:T(8,128)(2,1)} %copy.104), calls=%async_computation.1 | async-start | bytes 1048576 | tf_op jit(solution)/shard_map/all_to_all | solution.py:107
  (62 other events, 451.4 us)
